TPU v7x, 32 devices: a whole 2x2x4 slice. The times are simulated.
32 devices in a mesh: dp: 8 (over z, x), tensor: 4 (over y, core).
Axes of the slice: x: 2, y: 2, z: 4, core: 2. Of those that a mesh axis runs over, the one named last changes fastest.
Arguments:
- block_input: bfloat16 [16384, 768], P(('dp', 'tensor')), may hold values from -6 to 6
- output_grad: bfloat16 [16384, 768], P(('dp', 'tensor')), may hold values from -6 to 6
- lengths: int32 [8], P('dp'), may hold values from 1024 to 2048, as said below
- in_proj: float32 [768, 2, 1536], P('dp', None, 'tensor'), may hold values from -0.21875 to 0.21875
- step_proj: float32 [768, 24], P('dp', 'tensor'), may hold values from -0.21875 to 0.21875
- out_proj: float32 [768, 1536], P('dp', 'tensor'), may hold values from -0.15625 to 0.15625
- channel_params: float32 [6, 1536], P(None, 'tensor'), may hold values from -0.6 to 1.5
- head_params: float32 [3, 24], P(None, 'tensor'), may hold values from -6 to 2.31
- state_proj: float32 [768, 256], P(('dp', 'tensor')), may hold values from -0.21875 to 0.21875
- state_conv: float32 [256, 5], P(('dp', 'tensor')), may hold values from -0.5 to 0.5
- norm_gain: float32 [768], P(('dp', 'tensor')), may hold values from 0.5 to 1.5
- first_in_proj: float32 [768, 2, 1536], P('dp', None, 'tensor'), may hold values from -1200 to 1200
- first_step_proj: float32 [768, 24], P('dp', 'tensor'), may hold values from -1200 to 1200
- first_out_proj: float32 [768, 1536], P('dp', 'tensor'), may hold values from -1200 to 1200
- first_channel_params: float32 [6, 1536], P(None, 'tensor'), may hold values from -1200 to 1200
- first_head_params: float32 [3, 24], P(None, 'tensor'), may hold values from -1200 to 1200
- first_state_proj: float32 [768, 256], P(('dp', 'tensor')), may hold values from -1200 to 1200
- first_state_conv: float32 [256, 5], P(('dp', 'tensor')), may hold values from -1200 to 1200
- first_norm_gain: float32 [768], P(('dp', 'tensor')), may hold values from -1200 to 1200
- second_in_proj: float32 [768, 2, 1536], P('dp', None, 'tensor'), may hold values from 1000 to 100000
- second_step_proj: float32 [768, 24], P('dp', 'tensor'), may hold values from 1000 to 100000
- second_out_proj: float32 [768, 1536], P('dp', 'tensor'), may hold values from 1000 to 100000
- second_channel_params: float32 [6, 1536], P(None, 'tensor'), may hold values from 1000 to 100000
- second_head_params: float32 [3, 24], P(None, 'tensor'), may hold values from 1000 to 100000
- second_state_proj: float32 [768, 256], P(('dp', 'tensor')), may hold values from 1000 to 100000
- second_state_conv: float32 [256, 5], P(('dp', 'tensor')), may hold values from 1000 to 100000
- second_norm_gain: float32 [768], P(('dp', 'tensor')), may hold values from 1000 to 100000
Outputs:
- output: bfloat16 [16384, 768], P(('dp', 'tensor'))
- input_grad: float32 [16384, 768], P(('dp', 'tensor'))
- grad_in_proj: float32 [768, 2, 1536], P('dp', None, 'tensor')
- grad_step_proj: float32 [768, 24], P('dp', 'tensor')
- grad_out_proj: float32 [768, 1536], P('dp', 'tensor')
- grad_channel_params: float32 [6, 1536], P(None, 'tensor')
- grad_head_params: float32 [3, 24], P(None, 'tensor')
- grad_state_proj: float32 [768, 256], P(('dp', 'tensor'))
- grad_state_conv: float32 [256, 5], P(('dp', 'tensor'))
- grad_norm_gain: float32 [768], P(('dp', 'tensor'))
- new_first_in_proj: float32 [768, 2, 1536], P('dp', None, 'tensor')
- new_first_step_proj: float32 [768, 24], P('dp', 'tensor')
- new_first_out_proj: float32 [768, 1536], P('dp', 'tensor')
- new_first_channel_params: float32 [6, 1536], P(None, 'tensor')
- new_first_head_params: float32 [3, 24], P(None, 'tensor')
- new_first_state_proj: float32 [768, 256], P(('dp', 'tensor'))
- new_first_state_conv: float32 [256, 5], P(('dp', 'tensor'))
- new_first_norm_gain: float32 [768], P(('dp', 'tensor'))
- new_second_in_proj: float32 [768, 2, 1536], P('dp', None, 'tensor')
- new_second_step_proj: float32 [768, 24], P('dp', 'tensor')
- new_second_out_proj: float32 [768, 1536], P('dp', 'tensor')
- new_second_channel_params: float32 [6, 1536], P(None, 'tensor')
- new_second_head_params: float32 [3, 24], P(None, 'tensor')
- new_second_state_proj: float32 [768, 256], P(('dp', 'tensor'))
- new_second_state_conv: float32 [256, 5], P(('dp', 'tensor'))
- new_second_norm_gain: float32 [768], P(('dp', 'tensor'))
- update_in_proj: float32 [768, 2, 1536], P('dp', None, 'tensor')
- update_step_proj: float32 [768, 24], P('dp', 'tensor')
- update_out_proj: float32 [768, 1536], P('dp', 'tensor')
- update_channel_params: float32 [6, 1536], P(None, 'tensor')
- update_head_params: float32 [3, 24], P(None, 'tensor')
- update_state_proj: float32 [768, 256], P(('dp', 'tensor'))
- update_state_conv: float32 [256, 5], P(('dp', 'tensor'))
- update_norm_gain: float32 [768], P(('dp', 'tensor'))
- lamb_norms: float32 [2, 8], replicated
Inputs may be any that keep to these rules, and one draw needn't show every extreme that they name: `lengths`: some sequence has exactly 2048 live positions.
All inputs are finite; a program needn't handle non-finite values.
Results may differ from a plain program's by a relative error of at most 0.012.
The roundings to bfloat16 on the way count: a program that leaves them out, or rounds other values in their place, can miss the bound.
Values may be sent and summed in bfloat16 or wider, within the bound.
No kernel may reach another device: no remote copies, remote signals or barrier semaphores. Data moves between devices by JAX's collectives and lax.ppermute only.
A program may use at most 192 MiB of HBM per device.

v0:
```python
import jax
import jax.numpy as jnp
from jax import lax
from jax.sharding import PartitionSpec as P

STATE = 128
CONV = 4
SPAN = 256
LMAX = 2048
INNER = 1536
EPSILON = 1e-05
ADAM_EPSILON = 1e-06
DECAY = 0.5
BIAS_FIRST = 0.875
BIAS_SECOND = 0.875
RATE = 0.3
WEIGHT_DECAY = 0.01
HIGHEST = lax.Precision.HIGHEST


def rounded(values):
    return lax.optimization_barrier(values.astype(jnp.bfloat16)).astype(jnp.float32)


def contract(left, right, left_dim, right_dim):
    return lax.dot_general(
        left, right, (((left_dim,), (right_dim,)), ((), ())), preferred_element_type=jnp.float32
    )


def causal_conv(values, kernel, offsets):
    padded = jnp.pad(values, ((kernel.shape[0] - 1, 0), (0, 0)))
    summed = offsets[None, :] + jnp.zeros_like(values)
    for offset in range(kernel.shape[0]):
        summed = summed + kernel[offset][None, :] * padded[offset : offset + values.shape[0]]
    return jax.nn.silu(summed)


def ssd_scan(signal, b_rows, c_rows, step_size, log_rate):
    length, head_count, head_width = signal.shape
    blocks = length // SPAN
    decay_log = -jnp.exp(log_rate)[None, :] * step_size
    x_blocks = signal.reshape(blocks, SPAN, head_count, head_width)
    dt_blocks = step_size.reshape(blocks, SPAN, head_count)
    b_blocks = b_rows.reshape(blocks, SPAN, -1)
    c_blocks = c_rows.reshape(blocks, SPAN, -1)
    cumulative = jnp.cumsum(decay_log.reshape(blocks, SPAN, head_count), axis=1)
    intersection = jnp.einsum("cqn,ckn->cqk", c_blocks, b_blocks, precision=HIGHEST)
    causal = jnp.arange(SPAN)[:, None] >= jnp.arange(SPAN)[None, :]
    spread = cumulative[:, :, None, :] - cumulative[:, None, :, :]
    damping = jnp.exp(jnp.where(causal[None, :, :, None], spread, -jnp.inf))
    mixing = intersection[:, :, :, None] * damping * dt_blocks[:, None, :, :]
    within = jnp.einsum("cqkh,ckhp->cqhp", mixing, x_blocks, precision=HIGHEST)
    closing = cumulative[:, -1, :]
    weights_end = jnp.exp(closing[:, None, :] - cumulative) * dt_blocks
    states = jnp.einsum("ckh,ckhp,ckn->chpn", weights_end, x_blocks, b_blocks, precision=HIGHEST)

    def carry_step(carried, element):
        state_new, closing_new = element
        return (jnp.exp(closing_new)[:, None, None] * carried + state_new, carried)

    initial = jnp.zeros(states.shape[1:], jnp.float32)
    unused, entering = lax.scan(carry_step, initial, (states, closing))
    across = (
        jnp.einsum("cqn,chpn->cqhp", c_blocks, entering, precision=HIGHEST)
        * jnp.exp(cumulative)[..., None]
    )
    return (within + across).reshape(length, head_count, head_width)


def gate_mix(signal, b_rows, c_rows, step_raw, gate_raw, head_local):
    length = signal.shape[0]
    head_count = head_local.shape[1]
    step_size = jax.nn.softplus(step_raw + head_local[1][None, :])
    shaped = signal.reshape(length, head_count, -1)
    mixed = (
        ssd_scan(shaped, b_rows, c_rows, step_size, head_local[0])
        + head_local[2][None, :, None] * shaped
    )
    return mixed.reshape(length, -1) * jax.nn.silu(gate_raw)


def gate_blocks(signal, b_rows, c_rows, step_raw, gate_raw, head_local):

    def one_sequence(element):
        return gate_mix(element[0], element[1], element[2], element[3], element[4], head_local)

    return lax.map(one_sequence, (signal, b_rows, c_rows, step_raw, gate_raw))


def conv_signal(values, params):
    return jax.vmap(causal_conv, (0, None, None))(values, params[:CONV], params[CONV])


def conv_state(values, params):
    return jax.vmap(causal_conv, (0, None, None))(values, params[:, :CONV].T, params[:, CONV])


def lamb_parts(weight, gradient, first_old, second_old):
    first_new = DECAY * first_old + (1.0 - DECAY) * gradient
    second_new = DECAY * second_old + (1.0 - DECAY) * gradient * gradient
    direction = (
        first_new / BIAS_FIRST / (jnp.sqrt(second_new / BIAS_SECOND) + ADAM_EPSILON)
        + WEIGHT_DECAY * weight
    )
    return (first_new, second_new, direction)


def local(
    block_input,
    output_grad,
    lengths,
    in_proj,
    step_proj,
    out_proj,
    channel_params,
    head_params,
    state_proj,
    state_conv,
    norm_gain,
    first_in_proj,
    first_step_proj,
    first_out_proj,
    first_channel_params,
    first_head_params,
    first_state_proj,
    first_state_conv,
    first_norm_gain,
    second_in_proj,
    second_step_proj,
    second_out_proj,
    second_channel_params,
    second_head_params,
    second_state_proj,
    second_state_conv,
    second_norm_gain,
):
    tensor_count = lax.axis_size("tensor")
    own_count = block_input.shape[0]
    group_count = own_count * tensor_count
    sequence_count = lengths.shape[0]
    by_sequence = (sequence_count, LMAX, -1)
    inputs = block_input.astype(jnp.float32)
    shared = (
        lax.all_gather(state_proj, ("dp", "tensor"), axis=0, tiled=True),
        lax.all_gather(state_conv, ("dp", "tensor"), axis=0, tiled=True),
        lax.all_gather(norm_gain, ("dp", "tensor"), axis=0, tiled=True),
    )
    state_weight = shared[0].astype(jnp.bfloat16)
    conv_whole = shared[1]
    gain_whole = shared[2]
    in_weight, step_weight, out_weight = (
        lax.all_gather(in_proj.astype(jnp.bfloat16), "dp", axis=0, tiled=True),
        lax.all_gather(step_proj.astype(jnp.bfloat16), "dp", axis=0, tiled=True),
        lax.all_gather(out_proj.astype(jnp.bfloat16), "dp", axis=0, tiled=True),
    )
    scale = lax.rsqrt(jnp.mean(inputs * inputs, axis=-1, keepdims=True) + EPSILON)
    normed_own = (inputs * scale * gain_whole[None, :]).astype(jnp.bfloat16)
    normed = lax.all_gather(normed_own, "tensor", axis=0, tiled=True)
    gate_raw = contract(normed, in_weight[:, 0, :], 1, 0)
    signal_raw = contract(normed, in_weight[:, 1, :], 1, 0)
    state_raw = contract(normed, state_weight, 1, 0)
    step_raw = contract(normed, step_weight, 1, 0)
    signal_act, signal_back = jax.vjp(
        conv_signal, signal_raw.reshape(by_sequence), channel_params[: CONV + 1]
    )
    state_act, state_back = jax.vjp(conv_state, state_raw.reshape(by_sequence), conv_whole)
    signal = rounded(signal_act)
    b_rows = rounded(state_act[:, :, :STATE])
    c_rows = rounded(state_act[:, :, STATE:])
    mixer_inputs = (
        signal,
        b_rows,
        c_rows,
        step_raw.reshape(by_sequence),
        gate_raw.reshape(by_sequence),
        head_params,
    )
    gated, mixer_back = jax.vjp(gate_blocks, *mixer_inputs)
    squares = lax.psum(jnp.sum(gated * gated, axis=-1), "tensor")
    gate_scale = lax.rsqrt(squares / INNER + EPSILON)[:, :, None]
    gate_gain = channel_params[CONV + 1]
    normalized = gated * gate_scale
    merged = (normalized * gate_gain).astype(jnp.bfloat16).reshape(group_count, -1)
    branch = lax.psum_scatter(
        contract(merged, out_weight, 1, 1), "tensor", scatter_dimension=0, tiled=True
    )
    position_all = lax.axis_index("tensor") * own_count + jnp.arange(own_count, dtype=jnp.int32)
    sequence_of = position_all // LMAX
    length_of = jnp.sum(
        jnp.where(
            sequence_of[:, None] == jnp.arange(sequence_count, dtype=jnp.int32)[None, :],
            lengths[None, :],
            0,
        ),
        axis=1,
    )
    live_own = (position_all % LMAX < length_of).astype(jnp.float32)[:, None]
    output = (inputs + branch * live_own).astype(jnp.bfloat16)
    masked_grad = jnp.where(live_own > 0.5, output_grad, jnp.zeros_like(output_grad))
    grad_rows = lax.all_gather(masked_grad, "tensor", axis=0, tiled=True)
    in_back, step_back, out_back = (
        lax.all_gather(in_proj.astype(jnp.bfloat16), "dp", axis=0, tiled=True),
        lax.all_gather(step_proj.astype(jnp.bfloat16), "dp", axis=0, tiled=True),
        lax.all_gather(out_proj.astype(jnp.bfloat16), "dp", axis=0, tiled=True),
    )
    merged_grad = contract(grad_rows, out_back, 1, 0).reshape(by_sequence)
    out_grad = contract(grad_rows, merged, 0, 0)
    weighted = merged_grad * gate_gain
    gain_grad = jnp.sum(merged_grad * normalized, axis=(0, 1))
    products = lax.psum(jnp.sum(weighted * gated, axis=-1), "tensor")
    gated_grad = gate_scale * weighted - gated * gate_scale**3 * (products / INNER)[:, :, None]
    signal_grad, b_grad, c_grad, step_grad, gate_grad, head_grad = mixer_back(gated_grad)
    signal_raw_grad, kernel_grad = signal_back(signal_grad)
    state_raw_grad, conv_grad = state_back(jnp.concatenate([b_grad, c_grad], axis=-1))
    gate_low = gate_grad.reshape(group_count, -1).astype(jnp.bfloat16)
    signal_low = signal_raw_grad.reshape(group_count, -1).astype(jnp.bfloat16)
    step_low = step_grad.reshape(group_count, -1).astype(jnp.bfloat16)
    in_grad = jnp.stack(
        [contract(normed, gate_low, 0, 0), contract(normed, signal_low, 0, 0)], axis=1
    )
    step_weight_grad = contract(normed, step_low, 0, 0)
    normed_part = (
        contract(gate_low, in_back[:, 0, :], 1, 1)
        + contract(signal_low, in_back[:, 1, :], 1, 1)
        + contract(step_low, step_back, 1, 1)
    )
    normed_sum, state_sum = (
        lax.psum_scatter(normed_part, "tensor", scatter_dimension=0, tiled=True),
        lax.psum_scatter(
            state_raw_grad.reshape(group_count, -1), "tensor", scatter_dimension=0, tiled=True
        ),
    )
    state_low = state_sum.astype(jnp.bfloat16)
    normed_grad = normed_sum + contract(state_low, state_weight, 1, 1)
    state_weight_grad = contract(normed_own, state_low, 0, 0)
    gain_in_grad = jnp.sum(normed_grad * inputs * scale, axis=0)
    scaled_grad = normed_grad * gain_whole[None, :]
    input_grad = (
        output_grad.astype(jnp.float32)
        + scale * scaled_grad
        - inputs * scale**3 * jnp.mean(scaled_grad * inputs, axis=-1, keepdims=True)
    )
    channel_grad = jnp.concatenate([kernel_grad, gain_grad[None, :]], axis=0)
    in_sum, step_sum, out_sum = (
        lax.psum_scatter(in_grad, "dp", scatter_dimension=0, tiled=True),
        lax.psum_scatter(step_weight_grad, "dp", scatter_dimension=0, tiled=True),
        lax.psum_scatter(out_grad, "dp", scatter_dimension=0, tiled=True),
    )
    channel_sum, head_sum = lax.psum((channel_grad, head_grad), "dp")
    state_proj_sum, state_conv_sum, gain_sum = (
        lax.psum_scatter(state_weight_grad, ("dp", "tensor"), scatter_dimension=0, tiled=True),
        lax.psum_scatter(conv_grad, ("dp", "tensor"), scatter_dimension=0, tiled=True),
        lax.psum_scatter(gain_in_grad, ("dp", "tensor"), scatter_dimension=0, tiled=True),
    )
    masters = (
        in_proj,
        step_proj,
        out_proj,
        channel_params,
        head_params,
        state_proj,
        state_conv,
        norm_gain,
    )
    gradients = (
        in_sum,
        step_sum,
        out_sum,
        channel_sum,
        head_sum,
        state_proj_sum,
        state_conv_sum,
        gain_sum,
    )
    firsts = (
        first_in_proj,
        first_step_proj,
        first_out_proj,
        first_channel_params,
        first_head_params,
        first_state_proj,
        first_state_conv,
        first_norm_gain,
    )
    seconds = (
        second_in_proj,
        second_step_proj,
        second_out_proj,
        second_channel_params,
        second_head_params,
        second_state_proj,
        second_state_conv,
        second_norm_gain,
    )
    dp_copies = float(lax.axis_size("dp"))
    copies = (1.0, 1.0, 1.0, dp_copies, dp_copies, 1.0, 1.0, 1.0)
    first_list = []
    second_list = []
    directions = []
    partials = []
    for weight, gradient, first_old, second_old, copy_count in zip(
        masters, gradients, firsts, seconds, copies
    ):
        first_new, second_new, direction = lamb_parts(weight, gradient, first_old, second_old)
        first_list.append(first_new)
        second_list.append(second_new)
        directions.append(direction)
        partials.append(
            jnp.stack(
                [jnp.sum(weight * weight) / copy_count, jnp.sum(direction * direction) / copy_count]
            )
        )
    norm_totals = lax.psum(jnp.stack(partials, axis=1), ("dp", "tensor"))
    lamb_norms = jnp.sqrt(norm_totals)
    update_list = [
        -RATE * lamb_norms[0, position] / lamb_norms[1, position] * directions[position]
        for position in range(8)
    ]
    return (
        output,
        input_grad,
        in_sum,
        step_sum,
        out_sum,
        channel_sum,
        head_sum,
        state_proj_sum,
        state_conv_sum,
        gain_sum,
        first_list[0],
        first_list[1],
        first_list[2],
        first_list[3],
        first_list[4],
        first_list[5],
        first_list[6],
        first_list[7],
        second_list[0],
        second_list[1],
        second_list[2],
        second_list[3],
        second_list[4],
        second_list[5],
        second_list[6],
        second_list[7],
        update_list[0],
        update_list[1],
        update_list[2],
        update_list[3],
        update_list[4],
        update_list[5],
        update_list[6],
        update_list[7],
        lamb_norms,
    )


def solution(mesh):
    placed = (
        P(("dp", "tensor"), None),
        P(("dp", "tensor"), None),
        P("dp"),
        P("dp", None, "tensor"),
        P("dp", "tensor"),
        P("dp", "tensor"),
        P(None, "tensor"),
        P(None, "tensor"),
        P(("dp", "tensor"), None),
        P(("dp", "tensor"), None),
        P(("dp", "tensor")),
        P("dp", None, "tensor"),
        P("dp", "tensor"),
        P("dp", "tensor"),
        P(None, "tensor"),
        P(None, "tensor"),
        P(("dp", "tensor"), None),
        P(("dp", "tensor"), None),
        P(("dp", "tensor")),
        P("dp", None, "tensor"),
        P("dp", "tensor"),
        P("dp", "tensor"),
        P(None, "tensor"),
        P(None, "tensor"),
        P(("dp", "tensor"), None),
        P(("dp", "tensor"), None),
        P(("dp", "tensor")),
    )
    return jax.shard_map(
        local,
        mesh=mesh,
        in_specs=placed,
        out_specs=(
            P(("dp", "tensor"), None),
            P(("dp", "tensor"), None),
            P("dp", None, "tensor"),
            P("dp", "tensor"),
            P("dp", "tensor"),
            P(None, "tensor"),
            P(None, "tensor"),
            P(("dp", "tensor"), None),
            P(("dp", "tensor"), None),
            P(("dp", "tensor")),
            P("dp", None, "tensor"),
            P("dp", "tensor"),
            P("dp", "tensor"),
            P(None, "tensor"),
            P(None, "tensor"),
            P(("dp", "tensor"), None),
            P(("dp", "tensor"), None),
            P(("dp", "tensor")),
            P("dp", None, "tensor"),
            P("dp", "tensor"),
            P("dp", "tensor"),
            P(None, "tensor"),
            P(None, "tensor"),
            P(("dp", "tensor"), None),
            P(("dp", "tensor"), None),
            P(("dp", "tensor")),
            P("dp", None, "tensor"),
            P("dp", "tensor"),
            P("dp", "tensor"),
            P(None, "tensor"),
            P(None, "tensor"),
            P(("dp", "tensor"), None),
            P(("dp", "tensor"), None),
            P(("dp", "tensor")),
            P(),
        ),
        check_vma=False,
    )
```

profile of v0, /device:TPU:0, one launch (start us, length us, event | category | flops | bytes accessed | tf_op | source)
XLA Modules:
  0.0 971.0 jit_solution(7439061539372715546)
XLA Ops:
  8.2 42.0 %all-reduce.26 = f32[768]{0:T(1024)S(1)} all-reduce(f32[768]{0:T(1024)S(1)} %dynamic-update-slice), channel_id=1, replica_groups=mesh['dp'=8,'tensor'=4] {'dp','tensor'}, use_global_device_ids=true, to_apply=%add.26 | all-reduce | flops 768 | bytes 6144
  52.8 2.3 fusion.56
  57.8 40.9 %all_gather.27 = f32[256,5]{1,0:T(8,128)S(1)} all-gather(f32[8,5]{1,0:T(8,128)S(1)} %copy-done.72), channel_id=1, replica_groups=mesh['dp'=8,'tensor'=4] {'dp','tensor'}, dimensions={0}, use_global_device_ids=true | all-gather | bytes 5280 | tf_op jit(solution)/shard_map/all_gather | solution.py:146
  100.7 26.1 %all-gather = bf16[8,96,6]{1,2,0:T(8,128)(2,1)S(1)} all-gather(bf16[1,96,6]{1,2,0:T(8,128)(2,1)S(1)} %get-tuple-element.954), channel_id=1, replica_groups=mesh['dp'=8,'tensor'=4] {'dp'}, dimensions={0}, use_global_device_ids=true | all-gather | bytes 10368 | tf_op jit(solution)/shard_map/all_gather | solution.py:154
  128.2 40.5 %all_gather.30 = bf16[768,256]{1,0:T(8,128)(2,1)} all-gather(bf16[24,256]{1,0:T(8,128)(2,1)S(1)} %get-tuple-element.951), channel_id=1, replica_groups=mesh['dp'=8,'tensor'=4] {'dp','tensor'}, dimensions={0}, use_global_device_ids=true | all-gather | bytes 405504 | tf_op jit(solution)/shard_map/all_gather | solution.py:145
  169.8 2.9 fusion.130
  173.6 6.1 reduce-window.26
  183.1 2.9 fusion.74
  186.0 3.6 multiply_convert_fusion.1
  189.6 3.1 copy.255
  192.7 3.4 copy.316
  197.2 2.6 multiply_convert_fusion.2
  201.5 3.5 fusion.42
  206.3 18.3 %while.62 = (s32[]{:T(128)}, f32[6,64,128]{2,1,0:T(8,128)S(1)}, f32[8,6,64,128]{3,2,1,0:T(8,128)}, f32[8,6]{1,0:T(8,128)S(1)}, f32[8,6,1,1]{1,3,2,0:T(1,128)}, /...) while((s32[]{:T(128)}, f32[6,64,128]{2,1,0:T(8,128)S(1)}, ...), condition=%wide.region_4.5_spmd.clone, body=%wide.region_3.4_spmd.clone.sunk | while | flops 196611 | bytes 984808 | solution.py:63
  224.6 2.8 copy.253
  227.5 2.0 copy.315
  231.6 9.4 bitcast_add_fusion.3
  240.9 3.9 copy.257
  244.8 4.6 reshape.856
  249.5 3.5 copy.258
  253.0 7.6 multiply_reduce_fusion.8
  260.6 7.8 psum.35
  268.4 5.8 fusion.110
  274.3 60.4 %reduce-scatter.19.cloned.1.call-done = f32[96,384]{1,0:T(8,128)} async-done(((f32[768,384]{1,0:T(8,128)}), f32[96,384]{1,0:T(8,128)}) %reduce-scatter.19.cloned.1.call-update) | async-done | bytes 147472 | tf_op jit(solution)/shard_map/reduce_scatter | solution.py:248
  334.8 2.7 multiply_reduce_fusion.16
  337.4 31.6 %all_gather.33 = bf16[768,384]{1,0:T(8,128)(2,1)S(1)} all-gather(bf16[96,384]{1,0:T(8,128)(2,1)S(1)} %get-tuple-element.940), channel_id=1, replica_groups=mesh['dp'=8,'tensor'=4] {'dp'}, dimensions={0}, use_global_device_ids=true | all-gather | bytes 663552 | tf_op jit(solution)/shard_map/all_gather | solution.py:155
  369.0 7.5 fusion.31
  376.5 6.6 psum.36
  383.9 5.7 multiply_reduce_fusion.2
  391.2 3.1 fusion.36
  394.3 3.6 copy.259
  397.9 3.6 copy.260
  401.5 3.5 copy.318
  406.9 2.9 multiply_reduce_fusion.7
  409.9 16.4 %fusion.12 = (f32[8,256,6]{1,2,0:T(8,128)}, f32[8,256,6]{1,2,0:T(8,128)}, f32[8,256,6]{1,2,0:T(8,128)}, f32[8,256,256]{2,1,0:T(8,128)}) fusion(f32[8,256,6]{1,2,0:T(8,128)S(1)} %get-tuple-element.920, f32[8,256,6]{1,2,0:T(8,128)S(1)} %bitcast.370, f32[8,256,256]{2,1,0:T(8,128)S(1)} %copy-done.42, pred[256,256]{1,0:T(8,128)(4,1)S(1)} %copy-done.67, ...), kind=kOutput, calls=%fused_computation.24 | convolution fusion | flops 2456252416 | bytes 9224192 | tf_op jit(solution)/shard_map/transpose(jvp())/while/body/eval_jaxpr/cqkh,ckhp->cqhp/dot_general | solution.py:53
  426.4 2.9 fusion.39
  429.3 6.2 fusion.70
  436.9 26.4 %while.63 = (s32[]{:T(128)}, f32[6,64,128]{2,1,0:T(8,128)S(1)}, f32[8,6,64,128]{3,2,1,0:T(8,128)}, f32[8,6]{1,0:T(8,128)S(1)}, f32[8,6,64,128]{3,2,1,0:T(8,128)}...) while((s32[]{:T(128)}, f32[6,64,128]{2,1,0:T(8,128)S(1)}, ...), condition=%wide.region_12.13_spmd.clone, body=%wide.region_10.12_spmd.clone.sunk | while | flops 294916 | bytes 1180016 | solution.py:63
  463.3 8.4 fusion.69
  471.8 3.1 fusion.132
  479.0 2.4 multiply_reduce_fusion.11
  482.1 2.0 fusion.45
  484.2 4.1 multiply_reduce_fusion.1
  491.0 15.0 %reduce-window.28 = f32[8,6,2,128]{3,0,1,2:T(8,128)S(1)} reduce-window(f32[8,6,2,128]{3,0,1,2:T(8,128)S(1)} %copy.271, f32[]{:T(128)} %constant.337.clone.1), window={size=1x1x1x128 pad=0_0x0_0x0_0x0_127}, to_apply=%region_18.19 | reduce-window | flops 1560576 | bytes 98308 | tf_op jit(solution)/shard_map/reduce-window
  506.4 13.3 %bitcast_add_fusion.2 = f32[8,256,6,64]{1,3,2,0:T(8,128)S(1)} fusion(f32[8,256,6,64]{1,3,2,0:T(8,128)} %fusion.132, f32[8,256,6]{1,2,0:T(8,128)S(1)} %get-tuple-element.920, f32[8,256,6]{1,2,0:T(8,128)} %bitcast.368, f32[8,256,256]{2,1,0:T(8,128)} %copy-done.41, pred[256,256]{1,0:T(8,128)(4,1)} %iota_compare_fusion, f32[8,256,6,64]{1,3,2,0:T(8,128)} %copy-done.7, ...), kind=kOutput, calls=%fused_computation.57 | convolution fusion | flops 2430074880 | bytes 11747328 | tf_op jit(solution)/shard_map/transpose(jvp())/while/body/eval_jaxpr/cqkh,ckhp->cqhp/dot_general | solution.py:53
  519.8 3.5 copy.263
  523.2 4.5 reshape.858
  527.8 3.6 copy.264
  534.6 11.2 %multiply_reduce_fusion.5 = (f32[384]{0:T(512)}, f32[384]{0:T(512)}, f32[384]{0:T(512)}, f32[384]{0:T(512)}, f32[384]{0:T(512)}, /*index=5*/f32[1,2048,384]{2,1,0:T(8,128)S(1)}) fusion(f32[1,2048,384]{2,1,0:T(8,128)} %bitcast.333, f32[2048,384]{1,0:T(8,128)} %copy-done.4, f32[1,2048,384]{2,1,0:T(8,128)} %get-tuple-element.918, f32[1,2048,384]{2,1,0:T(8,128)} %copy.264, ...), kind=kLoop, calls=%fused_computation.76 | loop fusion | flops 19658880 | bytes 22029312 | tf_op jit(solution)/shard_map/transpose(jvp(vmap()))/reduce_sum | solution.py:35
  545.8 4.7 broadcast_multiply_fusion
  550.6 5.6 fusion.53
  563.1 4.5 fusion.73
  567.6 2.5 fusion.82
  572.0 6.5 add_add_fusion
  580.4 5.6 fusion.112
  591.3 35.5 %all-reduce.30 = (f32[6,384]{1,0:T(8,128)S(1)}, f32[3,6]{1,0:T(4,128)S(1)}) all-reduce(f32[6,384]{1,0:T(8,128)S(1)} %pad_maximum_fusion.2, f32[3,6]{1,0:T(4,128)S(1)} %pad_add_fusion.9), channel_id=1, replica_groups=mesh['dp'=8,'tensor'=4] {'dp'}, use_global_device_ids=true, to_apply=%region_33.34 | all-reduce | flops 2322 | bytes 18576 | tf_op jit(solution)/shard_map/psum | solution.py:250
  640.1 43.3 %reduce-scatter.17.cloned.1.call-done = f32[96,2,384]{2,0,1:T(8,128)} async-done(((f32[768,2,384]{2,0,1:T(8,128)}), f32[96,2,384]{2,0,1:T(8,128)}) %reduce-scatter.17.cloned.1.call-update) | async-done | bytes 294928 | tf_op jit(solution)/shard_map/reduce_scatter | solution.py:246
  683.5 2.5 multiply_reduce_fusion.13
  689.9 94.7 %reduce-scatter.21.cloned.1.call-done = f32[24,256]{1,0:T(8,128)} async-done(((f32[768,256]{1,0:T(8,128)}), f32[24,256]{1,0:T(8,128)}) %reduce-scatter.21.cloned.1.call-update) | async-done | bytes 24592 | tf_op jit(solution)/shard_map/reduce_scatter | solution.py:252
  788.5 56.2 %reduce-scatter.13.cloned.1.call-done = f32[512,768]{1,0:T(8,128)} async-done(((f32[2048,768]{1,0:T(8,128)}), f32[512,768]{1,0:T(8,128)}) %reduce-scatter.13.cloned.1.call-update) | async-done | bytes 1572880 | tf_op jit(solution)/shard_map/reduce_scatter | solution.py:229
  844.7 2.9 fusion.62
  847.6 39.9 %all-reduce.29 = (f32[256,5]{0,1:T(8,128)S(1)}, f32[768]{0:T(1024)S(1)}) all-reduce(f32[256,5]{0,1:T(8,128)} %pad_add_fusion.7, f32[768]{0:T(1024)} %get-tuple-element.823), channel_id=9, replica_groups=mesh['dp'=8,'tensor'=4] {'dp','tensor'}, use_global_device_ids=true, to_apply=%region_45.46.clone | all-reduce | flops 2048 | bytes 16384
  896.3 41.0 %psum.39 = f32[2,8]{1,0:T(2,128)S(1)} all-reduce(f32[2,8]{1,0:T(2,128)S(1)} %stack.143), channel_id=1, replica_groups=mesh['dp'=8,'tensor'=4] {'dp','tensor'}, use_global_device_ids=true, to_apply=%region_64.65 | all-reduce | flops 16 | bytes 128 | tf_op jit(solution)/shard_map/psum | solution.py:314
  960.5 3.4 fusion.59
  (496 shorter events, 136.4 us)
Async XLA Ops:
  7.2 47.9 %copy-start.38 = (f32[96,2,384]{2,1,0:T(2,128)S(1)}, f32[96,2,384]{2,1,0:T(2,128)}, u32[]{:S(2)}) copy-start(f32[96,2,384]{2,1,0:T(2,128)} %param.34) | copy-start | bytes 884740
  7.2 49.4 %copy-start.36 = (bf16[512,768]{1,0:T(8,128)(2,1)S(1)}, bf16[512,768]{1,0:T(8,128)(2,1)}, u32[]{:S(2)}) copy-start(bf16[512,768]{1,0:T(8,128)(2,1)} %param.32) | copy-start | bytes 2359300
  7.2 50.5 %copy-start.72 = (f32[8,5]{1,0:T(8,128)S(1)}, f32[8,5]{1,0:T(8,128)}, u32[]{:S(2)}) copy-start(f32[8,5]{1,0:T(8,128)} %param.40) | copy-start | bytes 484
  7.2 162.6 %all-gather.5.cloned.1.call-start = ((), (), s32[]{:S(2)}) async-start(), calls=%async_computation.7 | async-start | bytes 3932160 | tf_op jit(solution)/shard_map/all_gather | solution.py:159
  50.2 48.5 %copy-start.68 = (f32[768]{0:T(1024)}, f32[768]{0:T(1024)S(1)}, u32[]{:S(2)}) copy-start(f32[768]{0:T(1024)S(1)} %all-reduce.26) | copy-start | bytes 9220
  51.6 48.5 %copy-start.89 = (f32[96,6]{0,1:T(8,128)S(1)}, f32[96,6]{0,1:T(8,128)}, u32[]{:S(2)}) copy-start(f32[96,6]{0,1:T(8,128)} %param.35) | copy-start | bytes 6916
  51.6 75.3 %copy-start.111 = (f32[3,6]{1,0:T(4,128)S(1)}, f32[3,6]{1,0:T(4,128)}, u32[]{:S(2)}) copy-start(f32[3,6]{1,0:T(4,128)} %param.38) | copy-start | bytes 220
  51.6 75.3 %copy-start.70 = (f32[6,384]{1,0:T(8,128)S(1)}, f32[6,384]{1,0:T(8,128)}, u32[]{:S(2)}) copy-start(f32[6,384]{1,0:T(8,128)} %param.37) | copy-start | bytes 27652
  51.6 76.0 %copy-start.63 = (f32[24,256]{1,0:T(8,128)S(1)}, f32[24,256]{1,0:T(8,128)}, u32[]{:S(2)}) copy-start(f32[24,256]{1,0:T(8,128)} %param.39) | copy-start | bytes 73732
  55.1 128.0 %all-gather.7.cloned.1.call-start = ((), (), s32[]{:S(2)}) async-start(), calls=%async_computation.8 | async-start | bytes 1327104 | tf_op jit(solution)/shard_map/all_gather | solution.py:153
  55.9 212.5 %all-gather.9.cloned.1.call-start = ((), (), s32[]{:S(2)}) async-start(), calls=%async_computation.10 | async-start | bytes 3932160 | tf_op jit(solution)/shard_map/all_gather | solution.py:201
  57.7 277.1 %reduce-scatter.19.cloned.1.call-start = ((), (), s32[]{:S(2)}) async-start(), calls=%async_computation.14 | async-start | bytes 1327104 | tf_op jit(solution)/shard_map/reduce_scatter | solution.py:248
  126.9 45.8 %copy-start.61 = (bf16[768,6]{0,1:T(8,128)(2,1)}, bf16[768,6]{0,1:T(8,128)(2,1)S(1)}, u32[]{:S(2)}) copy-start(bf16[768,6]{0,1:T(8,128)(2,1)S(1)} %reshape.870) | copy-start | bytes 27652
  127.0 45.8 %copy-start.113 = (f32[6]{0:T(128)}, f32[6]{0:T(128)S(1)}, u32[]{:S(2)}) copy-start(f32[6]{0:T(128)S(1)} %get-tuple-element.959) | copy-start | bytes 76
  127.0 45.8 %copy-start.115 = (f32[6]{0:T(128)}, f32[6]{0:T(128)S(1)}, u32[]{:S(2)}) copy-start(f32[6]{0:T(128)S(1)} %get-tuple-element.960) | copy-start | bytes 76
  127.6 58.4 %copy-start.81 = (f32[384]{0:T(512)}, f32[384]{0:T(512)S(1)}, u32[]{:S(2)}) copy-start(f32[384]{0:T(512)S(1)} %get-tuple-element.832) | copy-start | bytes 4612
  127.6 256.2 %copy-start.74 = (f32[384]{0:T(512)}, f32[384]{0:T(512)S(1)}, u32[]{:S(2)}) copy-start(f32[384]{0:T(512)S(1)} %get-tuple-element.831) | copy-start | bytes 4612
  169.8 83.2 %copy-start.79 = (f32[384]{0:T(512)}, f32[384]{0:T(512)S(1)}, u32[]{:S(2)}) copy-start(f32[384]{0:T(512)S(1)} %mul.1038) | copy-start | bytes 4612
  169.8 13.3 %copy-start = (bf16[2048,768]{1,0:T(8,128)(2,1)S(1)}, bf16[2048,768]{1,0:T(8,128)(2,1)}, u32[]{:S(2)}) copy-start(bf16[2048,768]{1,0:T(8,128)(2,1)} %all-gather.5.cloned.1.call-done) | copy-start | bytes 9437188
  230.0 10.9 %copy-start.41 = (f32[8,256,256]{2,1,0:T(8,128)}, f32[8,256,256]{2,1,0:T(8,128)S(1)}, u32[]{:S(2)}) copy-start(f32[8,256,256]{2,1,0:T(8,128)S(1)} %fusion.129) | copy-start | bytes 6291460
  231.5 9.4 copy-start.24
  274.3 293.3 %reduce-scatter.15.cloned.1.call-start = ((), (), s32[]{:S(2)}) async-start(), calls=%async_computation.12 | async-start | bytes 2621440 | tf_op jit(solution)/shard_map/reduce_scatter | solution.py:230
  409.9 19.4 %copy-start.7 = (f32[8,256,6,64]{1,3,2,0:T(8,128)}, f32[8,256,6,64]{1,3,2,0:T(8,128)S(1)}, u32[]{:S(2)}) copy-start(f32[8,256,6,64]{1,3,2,0:T(8,128)S(1)} %get-tuple-element.914) | copy-start | bytes 9437188
  409.9 16.5 %copy-start.21 = (bf16[1,2048,128]{2,1,0:T(8,128)(2,1)S(1)}, bf16[1,2048,128]{2,1,0:T(8,128)(2,1)}, u32[]{:S(2)}) copy-start(bf16[1,2048,128]{2,1,0:T(8,128)(2,1)} %get-tuple-element.936) | copy-start | bytes 1572868
  409.9 16.5 %copy-start.49 = (f32[8,256,6]{1,2,0:T(8,128)S(1)}, f32[8,256,6]{1,2,0:T(8,128)}, u32[]{:S(2)}) copy-start(f32[8,256,6]{1,2,0:T(8,128)} %get-tuple-element.948) | copy-start | bytes 147460
  463.3 8.5 copy-start.12
  484.1 22.3 %copy-start.45 = (f32[8,256,6]{1,2,0:T(8,128)S(1)}, f32[8,256,6]{1,2,0:T(8,128)}, u32[]{:S(2)}) copy-start(f32[8,256,6]{1,2,0:T(8,128)} %copy-done.44) | copy-start | bytes 147460
  484.1 151.9 %reduce-scatter.23.cloned.1.call-start = ((), (), s32[]{:S(2)}) async-start(), calls=%async_computation.16 | async-start | bytes 442368
  506.1 13.7 %copy-start.46 = (f32[8,6,2,128]{3,0,1,2:T(8,128)}, f32[8,6,2,128]{3,0,1,2:T(8,128)S(1)}, u32[]{:S(2)}) copy-start(f32[8,6,2,128]{3,0,1,2:T(8,128)S(1)} %reduce-window.28) | copy-start | bytes 147460
  532.8 13.0 %copy-start.59 = (bf16[2048,6]{0,1:T(8,128)(2,1)}, bf16[2048,6]{0,1:T(8,128)(2,1)S(1)}, u32[]{:S(2)}) copy-start(bf16[2048,6]{0,1:T(8,128)(2,1)S(1)} %get-tuple-element.911) | copy-start | bytes 73732
  534.5 11.2 %copy-start.82 = (f32[384]{0:T(512)S(1)}, f32[384]{0:T(512)}, u32[]{:S(2)}) copy-start(f32[384]{0:T(512)} %copy-done.81) | copy-start | bytes 4612
  534.5 11.2 %copy-start.84 = (f32[384]{0:T(512)S(1)}, f32[384]{0:T(512)}, u32[]{:S(2)}) copy-start(f32[384]{0:T(512)} %get-tuple-element.833) | copy-start | bytes 4612
  534.5 11.2 %copy-start.86 = (f32[384]{0:T(512)S(1)}, f32[384]{0:T(512)}, u32[]{:S(2)}) copy-start(f32[384]{0:T(512)} %get-tuple-element.834) | copy-start | bytes 4612
  534.5 11.2 %copy-start.88 = (f32[384]{0:T(512)S(1)}, f32[384]{0:T(512)}, u32[]{:S(2)}) copy-start(f32[384]{0:T(512)} %get-tuple-element.835) | copy-start | bytes 4612
  550.6 132.9 %reduce-scatter.17.cloned.1.call-start = ((), (), s32[]{:S(2)}) async-start(), calls=%async_computation.13 | async-start | bytes 2654208 | tf_op jit(solution)/shard_map/reduce_scatter | solution.py:246
  561.7 222.9 %reduce-scatter.21.cloned.1.call-start = ((), (), s32[]{:S(2)}) async-start(), calls=%async_computation.15 | async-start | bytes 811008 | tf_op jit(solution)/shard_map/reduce_scatter | solution.py:252
  570.1 274.6 %reduce-scatter.13.cloned.1.call-start = ((), (), s32[]{:S(2)}) async-start(), calls=%async_computation.11 | async-start | bytes 7864320 | tf_op jit(solution)/shard_map/reduce_scatter | solution.py:229
  578.5 382.0 %reduce-scatter.11.cloned.1.call-start = ((), (), s32[]{:S(2)}) async-start(), calls=%async_computation.9 | async-start | bytes 7864320 | tf_op jit(solution)/shard_map/reduce_scatter | solution.py:185
  586.1 40.7 %copy-start.128 = (f32[3,6]{1,0:T(4,128)S(1)}, f32[3,6]{1,0:T(4,128)}, u32[]{:S(2)}) copy-start(f32[3,6]{1,0:T(4,128)} %param.54) | copy-start | bytes 220
  586.1 40.7 %copy-start.129 = (f32[3,6]{1,0:T(4,128)S(1)}, f32[3,6]{1,0:T(4,128)}, u32[]{:S(2)}) copy-start(f32[3,6]{1,0:T(4,128)} %param.46) | copy-start | bytes 220
  586.1 43.9 %copy-start.71 = (f32[6,384]{1,0:T(8,128)S(1)}, f32[6,384]{1,0:T(8,128)}, u32[]{:S(2)}) copy-start(f32[6,384]{1,0:T(8,128)} %param.37) | copy-start | bytes 27652
  586.1 43.9 %copy-start.92 = (f32[6,384]{1,0:T(8,128)S(1)}, f32[6,384]{1,0:T(8,128)}, u32[]{:S(2)}) copy-start(f32[6,384]{1,0:T(8,128)} %param.53) | copy-start | bytes 27652
  586.2 43.9 %copy-start.93 = (f32[6,384]{1,0:T(8,128)S(1)}, f32[6,384]{1,0:T(8,128)}, u32[]{:S(2)}) copy-start(f32[6,384]{1,0:T(8,128)} %param.45) | copy-start | bytes 27652
  586.2 49.2 %copy-start.119 = (f32[256]{0:T(256)S(1)}, f32[256]{0:T(256)}, u32[]{:S(2)}) copy-start(f32[256]{0:T(256)} %get-tuple-element.818) | copy-start | bytes 3076
  586.2 49.2 %copy-start.120 = (f32[256]{0:T(256)S(1)}, f32[256]{0:T(256)}, u32[]{:S(2)}) copy-start(f32[256]{0:T(256)} %get-tuple-element.819) | copy-start | bytes 3076
  586.2 49.1 %copy-start.121 = (f32[256]{0:T(256)S(1)}, f32[256]{0:T(256)}, u32[]{:S(2)}) copy-start(f32[256]{0:T(256)} %get-tuple-element.820) | copy-start | bytes 3076
  586.2 49.1 %copy-start.122 = (f32[256]{0:T(256)S(1)}, f32[256]{0:T(256)}, u32[]{:S(2)}) copy-start(f32[256]{0:T(256)} %get-tuple-element.826) | copy-start | bytes 3076
  586.2 49.1 %copy-start.118 = (f32[256]{0:T(256)S(1)}, f32[256]{0:T(256)}, u32[]{:S(2)}) copy-start(f32[256]{0:T(256)} %get-tuple-element.825) | copy-start | bytes 3076
  586.2 50.6 %copy-start.90 = (f32[96,6]{0,1:T(8,128)S(1)}, f32[96,6]{0,1:T(8,128)}, u32[]{:S(2)}) copy-start(f32[96,6]{0,1:T(8,128)} %param.35) | copy-start | bytes 6916
  586.2 50.6 %copy-start.123 = (f32[96,6]{0,1:T(8,128)S(1)}, f32[96,6]{0,1:T(8,128)}, u32[]{:S(2)}) copy-start(f32[96,6]{0,1:T(8,128)} %param.51) | copy-start | bytes 6916
  586.2 50.6 %copy-start.124 = (f32[96,6]{0,1:T(8,128)S(1)}, f32[96,6]{0,1:T(8,128)}, u32[]{:S(2)}) copy-start(f32[96,6]{0,1:T(8,128)} %param.43) | copy-start | bytes 6916
  586.3 97.2 %copy-start.51 = (f32[96,2,384]{2,1,0:T(2,128)S(1)}, f32[96,2,384]{2,1,0:T(2,128)}, u32[]{:S(2)}) copy-start(f32[96,2,384]{2,1,0:T(2,128)} %param.50) | copy-start | bytes 884740
  586.3 97.2 %copy-start.52 = (f32[96,2,384]{2,1,0:T(2,128)S(1)}, f32[96,2,384]{2,1,0:T(2,128)}, u32[]{:S(2)}) copy-start(f32[96,2,384]{2,1,0:T(2,128)} %param.42) | copy-start | bytes 884740
  586.3 198.2 %copy-start.64 = (f32[24,256]{1,0:T(8,128)S(1)}, f32[24,256]{1,0:T(8,128)}, u32[]{:S(2)}) copy-start(f32[24,256]{1,0:T(8,128)} %param.39) | copy-start | bytes 73732
  586.3 198.2 %copy-start.77 = (f32[24,256]{1,0:T(8,128)S(1)}, f32[24,256]{1,0:T(8,128)}, u32[]{:S(2)}) copy-start(f32[24,256]{1,0:T(8,128)} %param.55) | copy-start | bytes 73732
  586.3 198.2 %copy-start.78 = (f32[24,256]{1,0:T(8,128)S(1)}, f32[24,256]{1,0:T(8,128)}, u32[]{:S(2)}) copy-start(f32[24,256]{1,0:T(8,128)} %param.47) | copy-start | bytes 73732
  586.3 258.3 %copy-start.27 = (bf16[512,768]{1,0:T(8,128)(2,1)S(1)}, bf16[512,768]{1,0:T(8,128)(2,1)}, u32[]{:S(2)}) copy-start(bf16[512,768]{1,0:T(8,128)(2,1)} %param.31) | copy-start | bytes 2359300
  586.4 258.3 %copy-start.35 = (bf16[768,256]{1,0:T(8,128)(2,1)S(1)}, bf16[768,256]{1,0:T(8,128)(2,1)}, u32[]{:S(2)}) copy-start(bf16[768,256]{1,0:T(8,128)(2,1)} %all_gather.30) | copy-start | bytes 1179652
  586.4 258.3 %copy-start.69 = (f32[768]{0:T(1024)S(1)}, f32[768]{0:T(1024)}, u32[]{:S(2)}) copy-start(f32[768]{0:T(1024)} %copy-done.68) | copy-start | bytes 9220
  626.8 13.3 %copy-start.94 = (f32[6,384]{1,0:T(8,128)}, f32[6,384]{1,0:T(8,128)S(1)}, u32[]{:S(2)}) copy-start(f32[6,384]{1,0:T(8,128)S(1)} %get-tuple-element.869) | copy-start | bytes 27652
  626.8 13.3 %copy-start.130 = (f32[3,6]{1,0:T(4,128)}, f32[3,6]{1,0:T(4,128)S(1)}, u32[]{:S(2)}) copy-start(f32[3,6]{1,0:T(4,128)S(1)} %get-tuple-element.870) | copy-start | bytes 220
  636.9 151.7 %copy-start.91 = (f32[96,6]{0,1:T(8,128)}, f32[96,6]{0,1:T(8,128)S(1)}, u32[]{:S(2)}) copy-start(f32[96,6]{0,1:T(8,128)S(1)} %copy.311) | copy-start | bytes 6916
  788.5 172.0 %copy-start.37 = (bf16[512,768]{1,0:T(8,128)(2,1)S(1)}, bf16[512,768]{1,0:T(8,128)(2,1)}, u32[]{:S(2)}) copy-start(bf16[512,768]{1,0:T(8,128)(2,1)} %param.32) | copy-start | bytes 2359300
  937.4 26.5 %copy-start.65 = (f32[2,8]{1,0:T(2,128)}, f32[2,8]{1,0:T(2,128)S(1)}, u32[]{:S(2)}) copy-start(f32[2,8]{1,0:T(2,128)S(1)} %sqrt.35) | copy-start | bytes 196
  (78 other events, 255.8 us)
Sparse Core Ops, SparseCore 0:
  55.2 29.0 all-gather.4
  87.1 41.1 all-gather.6
  129.8 29.2 all-gather.8
  274.4 60.3 reduce-scatter.18
  484.2 30.5 reduce-scatter.14
  550.7 60.5 reduce-scatter.22
  615.2 68.1 reduce-scatter.16
  689.9 94.5 reduce-scatter.20
  787.2 57.4 reduce-scatter.12
  847.1 59.2 reduce-scatter.10
where the time goes:
time: 977 us; the launch traced here: 971 us
  blocking collectives  312 us (32%)
  waiting for transfers between devices  255 us (26%)
  other arithmetic  155 us (16%)
  matrix products  125 us (13%)
  local copies, waits for them, and re-layouts  92.9 us (10%)
  between operations  29.8 us (3%)
    reduce_scatter x1, waiting for transfers between devices, local(): lax.psum_scatter(state_weight_grad, ('dp', 'tensor'), scatter_dimension=0...  94.7 us
    unnamed x2, blocking collectives  81.9 us
    reduce_scatter x1, waiting for transfers between devices, local(): lax.psum_scatter(out_grad, 'dp', scatter_dimension=0, tiled=True)  60.4 us
    reduce_scatter x1, waiting for transfers between devices, local(): lax.psum_scatter(normed_part, 'tensor', scatter_dimension=0, tiled=True)  56.2 us
    dot_general x14, matrix products, contract(): lax.dot_general(left, right, (((left_dim,), (right_dim,)), ((), ())), pre...  55 us
    reduce_scatter x1, waiting for transfers between devices, local(): lax.psum_scatter(in_grad, 'dp', scatter_dimension=0, tiled=True)  43.3 us
    psum x1, blocking collectives, local(): norm_totals = lax.psum(jnp.stack(partials, axis=1), ('dp', 'tensor'))  41 us
    all_gather x1, blocking collectives, local(): lax.all_gather(state_conv, ('dp', 'tensor'), axis=0, tiled=True)  40.9 us
  transfers between devices with their start and end apart: 10, of which 4 were waited for; matrix products, arithmetic and copies ran while one was open for 25% of the time, Pallas kernels for 0%

commit v1 on v0

--- a/solution.py
+++ b/solution.py
@@ -16,6 +16,19 @@
 RATE = 0.3
 WEIGHT_DECAY = 0.01
 HIGHEST = lax.Precision.HIGHEST
+
+
+def collect(shard, axis, dim):
+    ways = lax.axis_size(axis)
+    up = [(d, (d + 1) % ways) for d in range(ways)]
+    down = [(d, (d - 1) % ways) for d in range(ways)]
+    earlier, later = ([shard], [shard])
+    for _ in range(ways // 2):
+        earlier.append(lax.ppermute(earlier[-1], axis, up))
+    for _ in range((ways - 1) // 2):
+        later.append(lax.ppermute(later[-1], axis, down))
+    line = jnp.concatenate([*earlier[::-1], *later[1:]], axis=dim)
+    return jnp.roll(line, (lax.axis_index(axis) - ways // 2) * shard.shape[dim], axis=dim)
 
 
 def rounded(values):
@@ -152,7 +165,7 @@
     in_weight, step_weight, out_weight = (
         lax.all_gather(in_proj.astype(jnp.bfloat16), "dp", axis=0, tiled=True),
         lax.all_gather(step_proj.astype(jnp.bfloat16), "dp", axis=0, tiled=True),
-        lax.all_gather(out_proj.astype(jnp.bfloat16), "dp", axis=0, tiled=True),
+        collect(out_proj.astype(jnp.bfloat16), "dp", 0),
     )
     scale = lax.rsqrt(jnp.mean(inputs * inputs, axis=-1, keepdims=True) + EPSILON)
     normed_own = (inputs * scale * gain_whole[None, :]).astype(jnp.bfloat16)

time: 977 us -> 985 us (level)
  starting transfers between devices: 0.42 us -> 14.9 us
  waiting for transfers between devices: 255 us -> 241 us
  local copies, waits for them, and re-layouts: 92.9 us -> 105 us
    reduce_scatter x1, waiting for transfers between devices: 43.3 us -> 14.3 us  [local(): lax.psum_scatter(in_grad, 'dp', scatter_dimension=0, tiled=True)]
    ppermute x0 -> x7, starting transfers between devices: none -> 14.5 us  [the longest x3 14.4 us: collect(): later.append(lax.ppermute(later[-1], axis, down))]
    ppermute x0 -> x7, waiting for transfers between devices: none -> 13.7 us  [the longest x4 13.7 us: collect(): earlier.append(lax.ppermute(earlier[-1], axis, up))]
    dynamic_update_slice x24, local copies, waits for them, and re-layouts: 4.67 us -> 14.8 us  [ssd_scan(): unused, entering = lax.scan(carry_step, initial, (states, closing))]
    unnamed x286 -> x291, local copies, waits for them, and re-layouts: 30.9 us -> 35 us
  transfers between devices with their start and end apart: 10 -> 17, of which waited for: 4 -> 8; matrix products, arithmetic and copies ran while one was open for 25% -> 25% of each run, Pallas kernels for 0% -> 0%
where the time goes in v1:
time: 985 us; the launch traced here: 979 us
  blocking collectives  310 us (31%)
  waiting for transfers between devices  241 us (24%)
  other arithmetic  153 us (16%)
  matrix products  125 us (13%)
  local copies, waits for them, and re-layouts  105 us (11%)
  between operations  29.9 us (3%)
  starting transfers between devices  14.9 us (2%)
    reduce_scatter x1, waiting for transfers between devices, local(): lax.psum_scatter(state_weight_grad, ('dp', 'tensor'), scatter_dimension=0...  95.9 us
    unnamed x2, blocking collectives  81.8 us
    reduce_scatter x1, waiting for transfers between devices, local(): lax.psum_scatter(out_grad, 'dp', scatter_dimension=0, tiled=True)  59.8 us
    reduce_scatter x1, waiting for transfers between devices, local(): lax.psum_scatter(normed_part, 'tensor', scatter_dimension=0, tiled=True)  56.8 us
    dot_general x14, matrix products, contract(): lax.dot_general(left, right, (((left_dim,), (right_dim,)), ((), ())), pre...  55.4 us
    psum x1, blocking collectives, local(): norm_totals = lax.psum(jnp.stack(partials, axis=1), ('dp', 'tensor'))  41.1 us
    all_gather x1, blocking collectives, local(): lax.all_gather(state_conv, ('dp', 'tensor'), axis=0, tiled=True)  40.9 us
    all_gather x1, blocking collectives, local(): lax.all_gather(state_proj, ('dp', 'tensor'), axis=0, tiled=True)  40.5 us
  transfers between devices with their start and end apart: 17, of which 8 were waited for; matrix products, arithmetic and copies ran while one was open for 25% of the time, Pallas kernels for 0%

profile of v1, /device:TPU:0, one launch (start us, length us, event | category | flops | bytes accessed | tf_op | source)
XLA Modules:
  0.0 979.2 jit_solution(16307056527182655911)
XLA Ops:
  8.2 42.0 %all-reduce.26 = f32[768]{0:T(1024)S(1)} all-reduce(f32[768]{0:T(1024)S(1)} %dynamic-update-slice), channel_id=1, replica_groups=mesh['dp'=8,'tensor'=4] {'dp','tensor'}, use_global_device_ids=true, to_apply=%add.26 | all-reduce | flops 768 | bytes 6144
  57.2 40.9 %all_gather.26 = f32[256,5]{1,0:T(8,128)S(1)} all-gather(f32[8,5]{1,0:T(8,128)S(1)} %copy-done.66), channel_id=1, replica_groups=mesh['dp'=8,'tensor'=4] {'dp','tensor'}, dimensions={0}, use_global_device_ids=true | all-gather | bytes 5280 | tf_op jit(solution)/shard_map/all_gather | solution.py:159
  100.1 26.1 %all-gather = bf16[8,96,6]{1,2,0:T(8,128)(2,1)S(1)} all-gather(bf16[1,96,6]{1,2,0:T(8,128)(2,1)S(1)} %get-tuple-element.954), channel_id=1, replica_groups=mesh['dp'=8,'tensor'=4] {'dp'}, dimensions={0}, use_global_device_ids=true | all-gather | bytes 10368 | tf_op jit(solution)/shard_map/all_gather | solution.py:167
  127.6 40.5 %all_gather.29 = bf16[768,256]{1,0:T(8,128)(2,1)} all-gather(bf16[24,256]{1,0:T(8,128)(2,1)S(1)} %get-tuple-element.951), channel_id=1, replica_groups=mesh['dp'=8,'tensor'=4] {'dp','tensor'}, dimensions={0}, use_global_device_ids=true | all-gather | bytes 405504 | tf_op jit(solution)/shard_map/all_gather | solution.py:158
  169.8 2.9 fusion.132
  173.5 6.1 reduce-window.26
  182.9 2.9 fusion.76
  185.9 3.6 multiply_convert_fusion.1
  189.5 3.0 copy.255
  192.5 3.4 copy.316
  197.0 2.6 multiply_convert_fusion.2
  201.3 3.5 fusion.42
  206.1 18.3 %while.62 = (s32[]{:T(128)}, f32[6,64,128]{2,1,0:T(8,128)S(1)}, f32[8,6,64,128]{3,2,1,0:T(8,128)}, f32[8,6]{1,0:T(8,128)S(1)}, f32[8,6,1,1]{1,3,2,0:T(1,128)}, /...) while((s32[]{:T(128)}, f32[6,64,128]{2,1,0:T(8,128)S(1)}, ...), condition=%wide.region_4.5_spmd.clone, body=%wide.region_3.4_spmd.clone.sunk | while | flops 196611 | bytes 984808 | solution.py:76
  224.4 2.8 copy.253
  231.4 9.4 bitcast_add_fusion.3
  240.8 3.8 copy.257
  244.6 4.6 reshape.856
  249.1 3.5 copy.258
  252.7 7.7 multiply_reduce_fusion.8
  260.3 7.8 psum.35
  268.2 5.8 fusion.113
  274.7 59.8 %reduce-scatter.19.cloned.1.call-done = f32[96,384]{1,0:T(8,128)} async-done(((f32[768,384]{1,0:T(8,128)}), f32[96,384]{1,0:T(8,128)}) %reduce-scatter.19.cloned.1.call-update) | async-done | bytes 147472 | tf_op jit(solution)/shard_map/reduce_scatter | solution.py:261
  334.5 2.6 multiply_reduce_fusion.16
  337.2 31.6 %all_gather.33 = bf16[768,384]{1,0:T(8,128)(2,1)S(1)} all-gather(bf16[96,384]{1,0:T(8,128)(2,1)S(1)} %get-tuple-element.940), channel_id=1, replica_groups=mesh['dp'=8,'tensor'=4] {'dp'}, dimensions={0}, use_global_device_ids=true | all-gather | bytes 663552 | tf_op jit(solution)/shard_map/all_gather | solution.py:218
  368.8 7.3 fusion.31
  376.0 6.6 psum.36
  383.4 5.7 multiply_reduce_fusion.2
  390.8 3.1 fusion.36
  393.9 3.6 copy.259
  397.5 3.6 copy.260
  401.2 3.5 copy.318
  406.5 2.9 multiply_reduce_fusion.7
  409.5 16.4 %fusion.12 = (f32[8,256,6]{1,2,0:T(8,128)}, f32[8,256,6]{1,2,0:T(8,128)}, f32[8,256,6]{1,2,0:T(8,128)}, f32[8,256,256]{2,1,0:T(8,128)}) fusion(f32[8,256,6]{1,2,0:T(8,128)S(1)} %get-tuple-element.920, f32[8,256,6]{1,2,0:T(8,128)S(1)} %bitcast.369, f32[8,256,256]{2,1,0:T(8,128)S(1)} %copy-done.40, pred[256,256]{1,0:T(8,128)(4,1)S(1)} %copy-done.61, ...), kind=kOutput, calls=%fused_computation.24 | convolution fusion | flops 2456252416 | bytes 9224192 | tf_op jit(solution)/shard_map/transpose(jvp())/while/body/eval_jaxpr/cqkh,ckhp->cqhp/dot_general | solution.py:66
  426.0 2.9 fusion.39
  428.9 6.2 fusion.70
  437.1 40.5 %while.63 = (s32[]{:T(128)}, f32[6,64,128]{2,1,0:T(8,128)S(1)}, f32[8,6,64,128]{3,2,1,0:T(8,128)}, f32[8,6]{1,0:T(8,128)}, f32[8,6,64,128]{3,2,1,0:T(8,128)}, /*...) while((s32[]{:T(128)}, f32[6,64,128]{2,1,0:T(8,128)S(1)}, ...), condition=%wide.region_12.13_spmd.clone, body=%wide.region_10.12_spmd.clone.sunk | while | flops 294916 | bytes 1180016 | solution.py:76
  477.6 8.4 fusion.69
  486.1 3.1 fusion.134
  493.3 2.4 multiply_reduce_fusion.11
  498.5 4.1 multiply_reduce_fusion.1
  505.3 15.0 %reduce-window.28 = f32[8,6,2,128]{3,0,1,2:T(8,128)S(1)} reduce-window(f32[8,6,2,128]{3,0,1,2:T(8,128)S(1)} %copy.271, f32[]{:T(128)} %constant.359.clone.1), window={size=1x1x1x128 pad=0_0x0_0x0_0x0_127}, to_apply=%region_18.19 | reduce-window | flops 1560576 | bytes 98308 | tf_op jit(solution)/shard_map/reduce-window
  520.7 13.4 %bitcast_add_fusion.2 = f32[8,256,6,64]{1,3,2,0:T(8,128)S(1)} fusion(f32[8,256,6,64]{1,3,2,0:T(8,128)} %fusion.134, f32[8,256,6]{1,2,0:T(8,128)S(1)} %get-tuple-element.920, f32[8,256,6]{1,2,0:T(8,128)} %bitcast.367, f32[8,256,256]{2,1,0:T(8,128)} %copy-done.39, pred[256,256]{1,0:T(8,128)(4,1)} %iota_compare_fusion, f32[8,256,6,64]{1,3,2,0:T(8,128)} %copy-done.7, ...), kind=kOutput, calls=%fused_computation.57 | convolution fusion | flops 2430074880 | bytes 11747328 | tf_op jit(solution)/shard_map/transpose(jvp())/while/body/eval_jaxpr/cqkh,ckhp->cqhp/dot_general | solution.py:66
  534.1 3.5 copy.263
  537.5 4.5 reshape.858
  542.1 3.6 copy.264
  548.4 11.0 %multiply_reduce_fusion.5 = (f32[384]{0:T(512)S(1)}, f32[384]{0:T(512)S(1)}, f32[384]{0:T(512)S(1)}, f32[384]{0:T(512)S(1)}, f32[384]{0:T(512)S(1)}, /*index=5*/f32[1,2048,384]{2,1,0:T(8,128)S(1)}) fusion(f32[1,2048,384]{2,1,0:T(8,128)} %bitcast.332, f32[2048,384]{1,0:T(8,128)} %copy-done.4, f32[1,2048,384]{2,1,0:T(8,128)} %get-tuple-element.918, ...), kind=kLoop, calls=%fused_computation.76 | loop fusion | flops 19658880 | bytes 22029312 | tf_op jit(solution)/shard_map/transpose(jvp(vmap()))/reduce_sum | solution.py:48
  559.4 4.8 broadcast_multiply_fusion
  564.3 5.6 fusion.53
  576.8 5.5 fusion.75
  582.3 2.5 fusion.84
  584.9 2.9 fusion.77
  587.7 6.5 add_add_fusion
  594.4 7.1 collective-permute-done
  601.5 4.7 collective-permute-start.4
  609.1 4.3 collective-permute-start.5
  615.7 5.4 collective-permute-start.6
  632.3 4.5 fusion.73
  639.8 34.0 %all-reduce.30 = (f32[6,384]{1,0:T(8,128)S(1)}, f32[3,6]{1,0:T(4,128)S(1)}) all-reduce(f32[6,384]{1,0:T(8,128)S(1)} %pad_maximum_fusion.2, f32[3,6]{1,0:T(4,128)S(1)} %pad_add_fusion.9), channel_id=1, replica_groups=mesh['dp'=8,'tensor'=4] {'dp'}, use_global_device_ids=true, to_apply=%region_33.34 | all-reduce | flops 2322 | bytes 18576 | tf_op jit(solution)/shard_map/psum | solution.py:263
  684.3 14.3 %reduce-scatter.17.cloned.1.call-done = f32[96,2,384]{2,0,1:T(8,128)} async-done(((f32[768,2,384]{2,0,1:T(8,128)}), f32[96,2,384]{2,0,1:T(8,128)}) %reduce-scatter.17.cloned.1.call-update) | async-done | bytes 294928 | tf_op jit(solution)/shard_map/reduce_scatter | solution.py:259
  703.8 95.9 %reduce-scatter.21.cloned.1.call-done = f32[24,256]{1,0:T(8,128)} async-done(((f32[768,256]{1,0:T(8,128)}), f32[24,256]{1,0:T(8,128)}) %reduce-scatter.21.cloned.1.call-update) | async-done | bytes 24592 | tf_op jit(solution)/shard_map/reduce_scatter | solution.py:265
  803.1 56.8 %reduce-scatter.13.cloned.1.call-done = f32[512,768]{1,0:T(8,128)} async-done(((f32[2048,768]{1,0:T(8,128)}), f32[512,768]{1,0:T(8,128)}) %reduce-scatter.13.cloned.1.call-update) | async-done | bytes 1572880 | tf_op jit(solution)/shard_map/reduce_scatter | solution.py:242
  862.2 39.8 %all-reduce.29 = (f32[256,5]{0,1:T(8,128)S(1)}, f32[768]{0:T(1024)S(1)}) all-reduce(f32[256,5]{0,1:T(8,128)S(1)} %pad_add_fusion.7, f32[768]{0:T(1024)S(1)} %get-tuple-element.823), channel_id=9, replica_groups=mesh['dp'=8,'tensor'=4] {'dp','tensor'}, use_global_device_ids=true, to_apply=%region_45.46.clone | all-reduce | flops 2048 | bytes 16384
  907.9 41.1 %psum.39 = f32[2,8]{1,0:T(2,128)S(1)} all-reduce(f32[2,8]{1,0:T(2,128)S(1)} %stack.143), channel_id=1, replica_groups=mesh['dp'=8,'tensor'=4] {'dp','tensor'}, use_global_device_ids=true, to_apply=%region_64.65 | all-reduce | flops 16 | bytes 128 | tf_op jit(solution)/shard_map/psum | solution.py:327
  968.4 3.7 fusion.59
  (516 shorter events, 161.4 us)
Async XLA Ops:
  7.2 47.3 %copy-start.37 = (f32[96,2,384]{2,1,0:T(2,128)S(1)}, f32[96,2,384]{2,1,0:T(2,128)}, u32[]{:S(2)}) copy-start(f32[96,2,384]{2,1,0:T(2,128)} %param.34) | copy-start | bytes 884740
  7.2 48.8 %copy-start.36 = (bf16[512,768]{1,0:T(8,128)(2,1)S(1)}, bf16[512,768]{1,0:T(8,128)(2,1)}, u32[]{:S(2)}) copy-start(bf16[512,768]{1,0:T(8,128)(2,1)} %param.32) | copy-start | bytes 2359300
  7.2 49.9 %copy-start.66 = (f32[8,5]{1,0:T(8,128)S(1)}, f32[8,5]{1,0:T(8,128)}, u32[]{:S(2)}) copy-start(f32[8,5]{1,0:T(8,128)} %param.40) | copy-start | bytes 484
  7.2 162.5 %all-gather.5.cloned.1.call-start = ((), (), s32[]{:S(2)}) async-start(), calls=%async_computation.7 | async-start | bytes 3932160 | tf_op jit(solution)/shard_map/all_gather | solution.py:172
  50.2 47.9 %copy-start.62 = (f32[768]{0:T(1024)}, f32[768]{0:T(1024)S(1)}, u32[]{:S(2)}) copy-start(f32[768]{0:T(1024)S(1)} %all-reduce.26) | copy-start | bytes 9220
  51.6 47.9 %copy-start.85 = (f32[96,6]{0,1:T(8,128)S(1)}, f32[96,6]{0,1:T(8,128)}, u32[]{:S(2)}) copy-start(f32[96,6]{0,1:T(8,128)} %param.35) | copy-start | bytes 6916
  51.6 74.7 %copy-start.104 = (f32[3,6]{1,0:T(4,128)S(1)}, f32[3,6]{1,0:T(4,128)}, u32[]{:S(2)}) copy-start(f32[3,6]{1,0:T(4,128)} %param.38) | copy-start | bytes 220
  51.6 74.7 %copy-start.64 = (f32[6,384]{1,0:T(8,128)S(1)}, f32[6,384]{1,0:T(8,128)}, u32[]{:S(2)}) copy-start(f32[6,384]{1,0:T(8,128)} %param.37) | copy-start | bytes 27652
  51.6 75.4 %copy-start.57 = (f32[24,256]{1,0:T(8,128)S(1)}, f32[24,256]{1,0:T(8,128)}, u32[]{:S(2)}) copy-start(f32[24,256]{1,0:T(8,128)} %param.39) | copy-start | bytes 73732
  52.2 47.9 %copy-start.68 = (f32[512]{0:T(512)}, f32[512]{0:T(512)S(1)}, u32[]{:S(2)}) copy-start(f32[512]{0:T(512)S(1)} %get-tuple-element.957) | copy-start | bytes 6148
  54.5 128.4 %all-gather.7.cloned.1.call-start = ((), (), s32[]{:S(2)}) async-start(), calls=%async_computation.8 | async-start | bytes 1327104 | tf_op jit(solution)/shard_map/all_gather | solution.py:166
  55.3 212.9 %all-gather.9.cloned.1.call-start = ((), (), s32[]{:S(2)}) async-start(), calls=%async_computation.10 | async-start | bytes 3932160 | tf_op jit(solution)/shard_map/all_gather | solution.py:214
  57.1 277.4 %reduce-scatter.19.cloned.1.call-start = ((), (), s32[]{:S(2)}) async-start(), calls=%async_computation.14 | async-start | bytes 1327104 | tf_op jit(solution)/shard_map/reduce_scatter | solution.py:261
  126.4 46.4 %copy-start.106 = (f32[6]{0:T(128)}, f32[6]{0:T(128)S(1)}, u32[]{:S(2)}) copy-start(f32[6]{0:T(128)S(1)} %get-tuple-element.959) | copy-start | bytes 76
  126.4 46.4 %copy-start.108 = (f32[6]{0:T(128)}, f32[6]{0:T(128)S(1)}, u32[]{:S(2)}) copy-start(f32[6]{0:T(128)S(1)} %get-tuple-element.960) | copy-start | bytes 76
  274.0 308.3 %reduce-scatter.15.cloned.1.call-start = ((), (), s32[]{:S(2)}) async-start(), calls=%async_computation.12 | async-start | bytes 2621440 | tf_op jit(solution)/shard_map/reduce_scatter | solution.py:243
  409.5 19.4 %copy-start.7 = (f32[8,256,6,64]{1,3,2,0:T(8,128)}, f32[8,256,6,64]{1,3,2,0:T(8,128)S(1)}, u32[]{:S(2)}) copy-start(f32[8,256,6,64]{1,3,2,0:T(8,128)S(1)} %get-tuple-element.914) | copy-start | bytes 9437188
  409.5 16.5 %copy-start.21 = (bf16[1,2048,128]{2,1,0:T(8,128)(2,1)S(1)}, bf16[1,2048,128]{2,1,0:T(8,128)(2,1)}, u32[]{:S(2)}) copy-start(bf16[1,2048,128]{2,1,0:T(8,128)(2,1)} %get-tuple-element.936) | copy-start | bytes 1572868
  498.4 22.3 %copy-start.45 = (f32[8,256,6]{1,2,0:T(8,128)S(1)}, f32[8,256,6]{1,2,0:T(8,128)}, u32[]{:S(2)}) copy-start(f32[8,256,6]{1,2,0:T(8,128)} %copy-done.44) | copy-start | bytes 147460
  498.4 182.3 %reduce-scatter.23.cloned.1.call-start = ((), (), s32[]{:S(2)}) async-start(), calls=%async_computation.16 | async-start | bytes 442368
  564.3 134.4 %reduce-scatter.17.cloned.1.call-start = ((), (), s32[]{:S(2)}) async-start(), calls=%async_computation.13 | async-start | bytes 2654208 | tf_op jit(solution)/shard_map/reduce_scatter | solution.py:259
  575.4 224.3 %reduce-scatter.21.cloned.1.call-start = ((), (), s32[]{:S(2)}) async-start(), calls=%async_computation.15 | async-start | bytes 811008 | tf_op jit(solution)/shard_map/reduce_scatter | solution.py:265
  584.8 275.1 %reduce-scatter.13.cloned.1.call-start = ((), (), s32[]{:S(2)}) async-start(), calls=%async_computation.11 | async-start | bytes 7864320 | tf_op jit(solution)/shard_map/reduce_scatter | solution.py:242
  594.3 38.1 %copy-start.9 = (f32[1,2048,384]{2,1,0:T(8,128)S(1)}, f32[1,2048,384]{2,1,0:T(8,128)}, u32[]{:S(2)}) copy-start(f32[1,2048,384]{2,1,0:T(8,128)} %get-tuple-element.916) | copy-start | bytes 9437188
  594.3 38.1 %copy-start.71 = (f32[384]{0:T(512)S(1)}, f32[384]{0:T(512)}, u32[]{:S(2)}) copy-start(f32[384]{0:T(512)} %get-tuple-element.831) | copy-start | bytes 4612
  594.3 374.1 %reduce-scatter.11.cloned.1.call-start = ((), (), s32[]{:S(2)}) async-start(), calls=%async_computation.9 | async-start | bytes 7864320 | tf_op jit(solution)/shard_map/reduce_scatter | solution.py:198
  594.3 7.1 collective-permute-start
  601.5 7.0 collective-permute-start.1
  601.5 7.1 collective-permute-start.4
  608.5 7.2 collective-permute-start.2
  609.1 6.6 collective-permute-start.5
  615.7 7.5 collective-permute-start.3
  615.7 12.0 %collective-permute-start.6 = (bf16[96,384]{1,0:T(8,128)(2,1)}, bf16[96,384]{1,0:T(8,128)(2,1)S(1)}, u32[]{:S(2)}, u32[]{:S(2)}) collective-permute-start(bf16[96,384]{1,0:T(8,128)(2,1)} %collective-permute-done.5), channel_id=1, source_target_pairs={{0,28},{4,0},{8,4},{12,8},{16,12},{20,16},{24,20},{28,24},{1,29},{... | collective-permute-start | bytes 221192 | tf_op jit(solution)/shard_map/ppermute | solution.py:29
  636.9 37.0 %copy-start.120 = (f32[3,6]{1,0:T(4,128)S(1)}, f32[3,6]{1,0:T(4,128)}, u32[]{:S(2)}) copy-start(f32[3,6]{1,0:T(4,128)} %param.54) | copy-start | bytes 220
  636.9 37.0 %copy-start.121 = (f32[3,6]{1,0:T(4,128)S(1)}, f32[3,6]{1,0:T(4,128)}, u32[]{:S(2)}) copy-start(f32[3,6]{1,0:T(4,128)} %param.46) | copy-start | bytes 220
  636.9 39.6 %copy-start.65 = (f32[6,384]{1,0:T(8,128)S(1)}, f32[6,384]{1,0:T(8,128)}, u32[]{:S(2)}) copy-start(f32[6,384]{1,0:T(8,128)} %param.37) | copy-start | bytes 27652
  637.0 39.6 %copy-start.89 = (f32[6,384]{1,0:T(8,128)S(1)}, f32[6,384]{1,0:T(8,128)}, u32[]{:S(2)}) copy-start(f32[6,384]{1,0:T(8,128)} %param.53) | copy-start | bytes 27652
  637.0 39.6 %copy-start.90 = (f32[6,384]{1,0:T(8,128)S(1)}, f32[6,384]{1,0:T(8,128)}, u32[]{:S(2)}) copy-start(f32[6,384]{1,0:T(8,128)} %param.45) | copy-start | bytes 27652
  637.0 43.7 %copy-start.112 = (f32[256]{0:T(256)S(1)}, f32[256]{0:T(256)}, u32[]{:S(2)}) copy-start(f32[256]{0:T(256)} %get-tuple-element.818) | copy-start | bytes 3076
  637.0 43.7 %copy-start.113 = (f32[256]{0:T(256)S(1)}, f32[256]{0:T(256)}, u32[]{:S(2)}) copy-start(f32[256]{0:T(256)} %get-tuple-element.819) | copy-start | bytes 3076
  637.0 43.6 %copy-start.114 = (f32[256]{0:T(256)S(1)}, f32[256]{0:T(256)}, u32[]{:S(2)}) copy-start(f32[256]{0:T(256)} %get-tuple-element.820) | copy-start | bytes 3076
  637.0 43.6 %copy-start.115 = (f32[256]{0:T(256)S(1)}, f32[256]{0:T(256)}, u32[]{:S(2)}) copy-start(f32[256]{0:T(256)} %get-tuple-element.826) | copy-start | bytes 3076
  637.0 43.7 %copy-start.111 = (f32[256]{0:T(256)S(1)}, f32[256]{0:T(256)}, u32[]{:S(2)}) copy-start(f32[256]{0:T(256)} %get-tuple-element.825) | copy-start | bytes 3076
  637.0 44.6 %copy-start.86 = (f32[96,6]{0,1:T(8,128)S(1)}, f32[96,6]{0,1:T(8,128)}, u32[]{:S(2)}) copy-start(f32[96,6]{0,1:T(8,128)} %param.35) | copy-start | bytes 6916
  637.1 44.6 %copy-start.116 = (f32[96,6]{0,1:T(8,128)S(1)}, f32[96,6]{0,1:T(8,128)}, u32[]{:S(2)}) copy-start(f32[96,6]{0,1:T(8,128)} %param.51) | copy-start | bytes 6916
  637.1 44.5 %copy-start.117 = (f32[96,6]{0,1:T(8,128)S(1)}, f32[96,6]{0,1:T(8,128)}, u32[]{:S(2)}) copy-start(f32[96,6]{0,1:T(8,128)} %param.43) | copy-start | bytes 6916
  637.1 61.5 %copy-start.48 = (f32[96,2,384]{2,1,0:T(2,128)S(1)}, f32[96,2,384]{2,1,0:T(2,128)}, u32[]{:S(2)}) copy-start(f32[96,2,384]{2,1,0:T(2,128)} %param.50) | copy-start | bytes 884740
  637.1 61.5 %copy-start.49 = (f32[96,2,384]{2,1,0:T(2,128)S(1)}, f32[96,2,384]{2,1,0:T(2,128)}, u32[]{:S(2)}) copy-start(f32[96,2,384]{2,1,0:T(2,128)} %param.42) | copy-start | bytes 884740
  637.1 162.6 %copy-start.58 = (f32[24,256]{1,0:T(8,128)S(1)}, f32[24,256]{1,0:T(8,128)}, u32[]{:S(2)}) copy-start(f32[24,256]{1,0:T(8,128)} %param.39) | copy-start | bytes 73732
  637.1 162.6 %copy-start.72 = (f32[24,256]{1,0:T(8,128)S(1)}, f32[24,256]{1,0:T(8,128)}, u32[]{:S(2)}) copy-start(f32[24,256]{1,0:T(8,128)} %param.55) | copy-start | bytes 73732
  637.2 162.5 %copy-start.73 = (f32[24,256]{1,0:T(8,128)S(1)}, f32[24,256]{1,0:T(8,128)}, u32[]{:S(2)}) copy-start(f32[24,256]{1,0:T(8,128)} %param.47) | copy-start | bytes 73732
  637.2 222.7 %copy-start.27 = (bf16[512,768]{1,0:T(8,128)(2,1)S(1)}, bf16[512,768]{1,0:T(8,128)(2,1)}, u32[]{:S(2)}) copy-start(bf16[512,768]{1,0:T(8,128)(2,1)} %param.31) | copy-start | bytes 2359300
  637.2 222.7 %copy-start.35 = (bf16[768,256]{1,0:T(8,128)(2,1)S(1)}, bf16[768,256]{1,0:T(8,128)(2,1)}, u32[]{:S(2)}) copy-start(bf16[768,256]{1,0:T(8,128)(2,1)} %all_gather.29) | copy-start | bytes 1179652
  637.2 222.7 %copy-start.63 = (f32[768]{0:T(1024)S(1)}, f32[768]{0:T(1024)}, u32[]{:S(2)}) copy-start(f32[768]{0:T(1024)} %copy-done.62) | copy-start | bytes 9220
  637.2 222.7 %copy-start.69 = (f32[512]{0:T(512)S(1)}, f32[512]{0:T(512)}, u32[]{:S(2)}) copy-start(f32[512]{0:T(512)} %copy-done.68) | copy-start | bytes 6148
  673.9 188.3 %copy-start.91 = (f32[6,384]{1,0:T(8,128)}, f32[6,384]{1,0:T(8,128)S(1)}, u32[]{:S(2)}) copy-start(f32[6,384]{1,0:T(8,128)S(1)} %get-tuple-element.869) | copy-start | bytes 27652
  673.9 188.3 %copy-start.122 = (f32[3,6]{1,0:T(4,128)}, f32[3,6]{1,0:T(4,128)S(1)}, u32[]{:S(2)}) copy-start(f32[3,6]{1,0:T(4,128)S(1)} %get-tuple-element.870) | copy-start | bytes 220
  681.6 180.6 %copy-start.88 = (f32[96,6]{0,1:T(8,128)}, f32[96,6]{0,1:T(8,128)S(1)}, u32[]{:S(2)}) copy-start(f32[96,6]{0,1:T(8,128)S(1)} %copy.311) | copy-start | bytes 6916
  700.4 201.6 %copy-start.124 = (f32[24]{0:T(128)S(1)}, f32[24]{0:T(128)}, u32[]{:S(2)}) copy-start(f32[24]{0:T(128)} %param.41) | copy-start | bytes 292
  700.4 201.6 %copy-start.125 = (f32[24]{0:T(128)S(1)}, f32[24]{0:T(128)}, u32[]{:S(2)}) copy-start(f32[24]{0:T(128)} %param.57) | copy-start | bytes 292
  700.4 201.6 %copy-start.126 = (f32[24]{0:T(128)S(1)}, f32[24]{0:T(128)}, u32[]{:S(2)}) copy-start(f32[24]{0:T(128)} %param.49) | copy-start | bytes 292
  701.9 205.0 %copy-start.41 = (f32[96,2,384]{2,0,1:T(8,128)S(1)}, f32[96,2,384]{2,0,1:T(8,128)}, u32[]{:S(2)}) copy-start(f32[96,2,384]{2,0,1:T(8,128)} %reduce-scatter.17.cloned.1.call-done) | copy-start | bytes 884740
  803.1 165.3 %copy-start.102 = (f32[512]{0:T(512)S(1)}, f32[512]{0:T(512)}, u32[]{:S(2)}) copy-start(f32[512]{0:T(512)} %get-tuple-element.956) | copy-start | bytes 6148
  948.9 23.1 %copy-start.59 = (f32[2,8]{1,0:T(2,128)}, f32[2,8]{1,0:T(2,128)S(1)}, u32[]{:S(2)}) copy-start(f32[2,8]{1,0:T(2,128)S(1)} %sqrt.35) | copy-start | bytes 196
  (80 other events, 339.1 us)
Sparse Core Ops, SparseCore 0:
  54.6 29.0 all-gather.4
  86.5 41.1 all-gather.6
  129.2 29.2 all-gather.8
  274.2 60.3 reduce-scatter.18
  498.5 30.5 reduce-scatter.14
  564.4 61.3 reduce-scatter.22
  629.6 68.9 reduce-scatter.16
  705.1 94.5 reduce-scatter.20
  802.4 57.4 reduce-scatter.12
  862.3 59.5 reduce-scatter.10
